TPU v7x, 256 devices: a whole 4x4x8 slice. The times are simulated.
256 devices in a mesh: video: 4 (over x), tm: 16 (over z, core), space: 4 (over y).
Axes of the slice: x: 4, y: 4, z: 8, core: 2. Of those that a mesh axis runs over, the one named last changes fastest.
Arguments:
- feature_maps: bfloat16 [64, 128, 240, 128], P(('video', 'tm'), 'space'), parts along dimension 0, may hold values from -27 to 27
- query_frame: int32 [2048], P('video'), parts along dimension 0, may hold values from 0 to 15
- query_row: int32 [2048], P('video'), parts along dimension 0, may hold values from 0 to 127
- query_col: int32 [2048], P('video'), parts along dimension 0, may hold values from 0 to 239
- ema_decay: float32 [64, 128], P(('video', 'tm')), parts along dimension 0, may hold values from 0.14 to 1
- dw_kernel: float32 [3, 128], replicated, may hold values from -3 to 3
- pw_weight: bfloat16 [128, 128], replicated, may hold values from -0.5 to 0.5
- out_weight: float32 [2, 128], replicated, may hold values from -2 to 2
Outputs:
- tracks: float32 [64, 2, 512], P(('video', 'tm')), parts along dimension 0
There are 4 independent parts, one for each index of `video`. A program takes and returns all parts, laid end to end along the dimension named above; an argument that names none is the same for every part. Nothing has to cross between parts.
All inputs are finite; a program needn't handle non-finite values.
Results may differ from a plain program's by a relative error of at most 0.0026.
Values may be sent and summed in bfloat16 or wider, within the bound.
A program may use at most 128 MiB of HBM per device.

v0:
```python
import math
import jax
import jax.numpy as jnp
from jax import lax
from jax.sharding import PartitionSpec as P


def with_halo(cells, sides, width):
    for axis, dim in sides:
        count = lax.axis_size(axis)
        ends = count - 1
        head = lax.slice_in_dim(cells, 0, width, axis=dim)
        tail = lax.slice_in_dim(cells, cells.shape[dim] - width, cells.shape[dim], axis=dim)
        cells = jnp.concatenate(
            [
                lax.ppermute(tail, axis, [(i, (i + 1) % count) for i in range(ends)]),
                cells,
                lax.ppermute(head, axis, [((i + 1) % count, i) for i in range(ends)]),
            ],
            axis=dim,
        )
    return cells


def local(
    feature_maps, query_frame, query_row, query_col, ema_decay, dw_kernel, pw_weight, out_weight
):
    frames_here, rows_here, map_width, channels = feature_maps.shape
    num_queries = query_frame.shape[0]
    first_frame = lax.axis_index("tm") * frames_here
    first_row = lax.axis_index("space") * rows_here
    map_height = rows_here * lax.axis_size("space")
    local_frame = query_frame - first_frame
    local_row = query_row - first_row
    owned = (
        (local_frame >= 0)
        & (local_frame < frames_here)
        & (local_row >= 0)
        & (local_row < rows_here)
    )
    picked = feature_maps[
        jnp.clip(local_frame, 0, frames_here - 1), jnp.clip(local_row, 0, rows_here - 1), query_col
    ]
    contrib = jnp.where(owned[:, None], picked.astype(jnp.float32), 0.0)
    query_feats = lax.psum(contrib, ("tm", "space")).astype(jnp.bfloat16)
    scale = 1.0 / math.sqrt(channels)
    col_coord = jnp.arange(map_width, dtype=jnp.int32).astype(jnp.float32) / map_width
    row_coord = (first_row + jnp.arange(rows_here, dtype=jnp.int32)).astype(
        jnp.float32
    ) / map_height
    highest_list, total_list, pos_list, feat_list = ([], [], [], [])
    frame_index = 0
    frame_map = feature_maps[frame_index].reshape(rows_here * map_width, channels)
    scores = (
        lax.dot_general(
            query_feats, frame_map, (((1,), (1,)), ((), ())), preferred_element_type=jnp.float32
        )
        * scale
    )
    highest = jnp.max(scores, axis=1)
    weights_exp = jnp.exp(scores - highest[:, None])
    highest_list.append(highest)
    total_list.append(jnp.sum(weights_exp, axis=1))
    grid = weights_exp.reshape(num_queries, rows_here, map_width)
    col_part = jnp.sum(jnp.sum(grid, axis=1) * col_coord[None, :], axis=1)
    line_portion = jnp.sum(jnp.sum(grid, axis=2) * row_coord[None, :], axis=1)
    pos_list.append(jnp.stack([col_part, line_portion], 1))
    feat_list.append(
        jnp.dot(weights_exp.astype(jnp.bfloat16), frame_map, preferred_element_type=jnp.float32)
    )
    highest = jnp.stack(highest_list)
    totals = jnp.stack(total_list)
    pos_sum = jnp.stack(pos_list)
    feat_sum = jnp.stack(feat_list)
    top_value = lax.pmax(highest, "space")
    factor = jnp.exp(highest - top_value)
    grand_total, pos_all, feat_all = lax.psum(
        (factor * totals, factor[..., None] * pos_sum, factor[..., None] * feat_sum), "space"
    )
    position = pos_all / grand_total[..., None]
    focused_result = (feat_all / grand_total[..., None]).astype(jnp.bfloat16)
    padded = with_halo(focused_result, (("tm", 0),), 1).astype(jnp.float32)
    depth = jnp.zeros((frames_here, num_queries, channels), jnp.float32)
    for tap in range(dw_kernel.shape[0]):
        depth = depth + dw_kernel[tap][None, None, :] * padded[tap : tap + frames_here]
    hidden = jax.nn.gelu(depth).astype(jnp.bfloat16)
    mixed = jnp.dot(
        hidden.reshape(-1, channels), pw_weight, preferred_element_type=jnp.float32
    ).reshape(frames_here, num_queries, channels)
    refined = focused_result.astype(jnp.float32) + mixed
    carried = jnp.zeros((num_queries, channels), jnp.float32)
    retain_prod = jnp.ones((channels,), jnp.float32)
    local_states, local_prods = ([], [])
    frame_index = 0
    retain = ema_decay[frame_index]
    carried = retain[None, :] * carried + (1.0 - retain[None, :]) * refined[frame_index]
    retain_prod = retain_prod * retain
    local_states.append(carried)
    local_prods.append(retain_prod)
    all_prods, all_ends = (
        lax.all_gather(retain_prod[None], "tm", axis=0, tiled=True),
        lax.all_gather(carried[None], "tm", axis=0, tiled=True),
    )
    position_tm = lax.axis_index("tm")

    def fold_step(source, running):
        advanced = all_prods[source][None, :] * running + all_ends[source]
        return jnp.where(source < position_tm, advanced, running)

    incoming = lax.fori_loop(
        0, lax.axis_size("tm"), fold_step, jnp.zeros((num_queries, channels), jnp.float32)
    )
    memory = jnp.stack(local_states) + jnp.stack(local_prods)[:, None, :] * incoming[None]
    delta = jnp.einsum("tqc,kc->tkq", memory, out_weight, precision=lax.Precision.HIGHEST)
    return jnp.transpose(position, (0, 2, 1)) + delta


def solution(mesh):
    placed = (
        P(("video", "tm"), "space", None, None),
        P("video"),
        P("video"),
        P("video"),
        P(("video", "tm"), None),
        P(),
        P(),
        P(),
    )
    return jax.shard_map(
        local, mesh=mesh, in_specs=placed, out_specs=P(("video", "tm"), None, None), check_vma=False
    )
```

profile of v0, /device:TPU:1, one launch (start us, length us, event | category | flops | bytes accessed | tf_op | source)
XLA Modules:
  0.0 416.0 jit_solution(9454271297745757524)
XLA Ops:
  6.5 0.0 copy-start
  6.5 0.0 all-reduce.4.cloned.1.call-start
  6.5 0.8 compare_and_fusion
  7.4 0.7 fusion.41
  8.1 0.0 copy-done
  8.1 3.1 gather_fusion
  11.3 0.1 convert_select_fusion
  11.4 250.4 %all-reduce.5 = bf16[512,128]{1,0:T(8,128)(2,1)S(1)} all-reduce(f32[512,128]{1,0:T(8,128)S(1)} %convert_select_fusion), channel_id=1, replica_groups=mesh['video'=4,'tm'=16,'space'=4] {'tm','space'}, use_global_device_ids=true, to_apply=%region_0.1 | all-reduce | flops 65536 | bytes 393216 | tf_op jit(solution)/shard_map/psum | solution.py:45
  261.8 2.3 multiply_reduce_fusion
  264.1 7.0 %fusion.50 = (f32[512]{0:T(512)S(1)}, f32[512,7680]{1,0:T(8,128)}) fusion(f32[512]{0:T(512)S(1)} %get-tuple-element.139, f32[512,7680]{1,0:T(8,128)S(1)} %get-tuple-element.140), kind=kLoop, calls=%fused_computation.74 | loop fusion | flops 11795968 | bytes 31461376 | tf_op jit(solution)/shard_map/reduce_sum | solution.py:63
  271.1 6.0 %pmax.7 = f32[1,512]{1,0:T(1,128)S(1)} all-reduce(f32[1,512]{1,0:T(1,128)S(1)} %bitcast.66), channel_id=1, replica_groups=mesh['video'=4,'tm'=16,'space'=4] {'space'}, use_global_device_ids=true, to_apply=%region_2.3 | all-reduce | flops 512 | bytes 4096 | tf_op jit(solution)/shard_map/pmax | solution.py:75
  277.1 8.4 %fusion.7 = f32[1,512,128]{2,1,0:T(8,128)} fusion(bf16[7680,128]{1,0:T(8,128)(2,1)S(1)} %bitcast.62, f32[512,7680]{1,0:T(8,128)} %get-tuple-element.135, f32[512]{0:T(512)S(1)} %bitcast.64), kind=kOutput, calls=%fused_computation.11 | convolution fusion | flops 1010630656 | bytes 17958912 | tf_op jit(solution)/shard_map/dot_general | solution.py:69
  285.5 0.0 all-reduce.4.cloned.1.call-update
  285.5 0.0 all-gather.3.cloned.1.call-start
  285.5 15.7 %copy.10 = f32[512,7680]{0,1:T(8,128)} copy(f32[512,7680]{1,0:T(8,128)} %get-tuple-element.135) | data formatting | bytes 31457280 | tf_op jit(solution)/shard_map/exp | solution.py:61
  301.3 0.0 copy-start.1
  301.3 0.0 copy-start.2
  301.3 0.0 copy-start.4
  301.3 0.0 copy-start.3
  301.3 7.9 %fusion.48 = (f32[512,240]{0,1:T(8,128)S(1)}, f32[512,32]{0,1:T(8,128)S(1)}) fusion(f32[512,32,240]{0,2,1:T(8,128)} %bitcast.63), kind=kLoop, calls=%fused_computation.72 | loop fusion | flops 7725056 | bytes 16285696 | tf_op jit(solution)/shard_map/reduce_sum | solution.py:65
  309.2 0.1 multiply_reduce_fusion.2
  309.3 0.1 multiply_reduce_fusion.1
  309.4 0.0 copy-done.1
  309.4 7.5 %all-reduce = (f32[512]{0:T(512)S(1)}, f32[1,512,2]{1,2,0:T(2,128)S(1)}) all-reduce(f32[512]{0:T(512)S(1)} %bitcast.70, f32[1,512,2]{1,2,0:T(2,128)S(1)} %maximum_multiply_fusion), channel_id=1, replica_groups=mesh['video'=4,'tm'=16,'space'=4] {'space'}, use_global_device_ids=true, to_apply=%region_9.10 | all-reduce | flops 1536 | bytes 12288 | tf_op jit(solution)/shard_map/psum | solution.py:77
  317.0 0.0 copy-done.2
  317.0 15.6 %all-reduce.4.cloned.1.call-done = f32[1,512,128]{2,1,0:T(8,128)} async-done(((f32[1,512,128]{2,1,0:T(8,128)}), f32[1,512,128]{2,1,0:T(8,128)}) %all-reduce.4.cloned.1.call-update) | async-done | bytes 262160 | tf_op jit(solution)/shard_map/psum | solution.py:77
  332.6 1.1 divide_convert_fusion
  333.7 4.7 %collective-permute-start.1 = (bf16[1,512,128]{2,1,0:T(8,128)(2,1)S(1)}, bf16[1,512,128]{2,1,0:T(8,128)(2,1)S(1)}, u32[]{:S(2)}, u32[]{:S(2)}) collective-permute-start(bf16[1,512,128]{2,1,0:T(8,128)(2,1)S(1)} %divide_convert_fusion), channel_id=1, source_target_pairs={{4,0},{8,4},{12,8},{16,12},{20,16},{24,20},{28,24},{32,28},{36,32}... | collective-permute-start | bytes 393224 | tf_op jit(solution)/shard_map/ppermute | solution.py:18
  338.4 3.1 collective-permute-start
  341.5 0.7 collective-permute-done.1
  342.2 1.2 collective-permute-done
  343.4 0.1 maximum_convert_fusion
  343.5 0.0 copy-done.4
  343.5 0.9 multiply_add_fusion
  344.4 0.0 all-gather.3.cloned.1.call-update
  344.5 18.6 %all-gather = f32[16,1,128]{2,1,0:T(1,128)S(1)} all-gather(f32[1,1,128]{2,1,0:T(1,128)S(1)} %bitcast.73), channel_id=1, replica_groups=mesh['video'=4,'tm'=16,'space'=4] {'tm'}, dimensions={0}, use_global_device_ids=true | all-gather | bytes 8704 | tf_op jit(solution)/shard_map/all_gather | solution.py:101
  363.0 26.2 %all-gather.3.cloned.1.call-done = f32[16,512,128]{2,1,0:T(8,128)} async-done(((f32[1,512,128]{2,1,0:T(8,128)}), f32[16,512,128]{2,1,0:T(8,128)}) %all-gather.3.cloned.1.call-update) | async-done | bytes 4194320 | tf_op jit(solution)/shard_map/all_gather | solution.py:102
  389.2 19.0 %while.14 = (s32[]{:T(128)}, f32[512,128]{1,0:T(8,128)S(1)}, s32[]{:T(128)}, f32[16,128]{1,0:T(8,128)S(1)}, f32[16,512,128]{2,1,0:T(8,128)}, /*index=5*/s32[]{:T(128)}, s32[]{:T(128)}) while((s32[]{:T(128)}, f32[512,128]{1,0:T(8,128)S(1)}, s32[]{:T(128)}, f32[16,128]{1,0:T(8,128)S(1)}, f32[16,512,128]{2,1,0:T(8,128)}, ...), condition=%wide.region_12.13_spmd.clone, body=%wide.region_11.12_spmd.clone.sunk | while | flops 262148 | bytes 788081 | solution.py:110
  389.2 1.1 fusion.57
  390.4 1.1 fusion.57
  391.6 1.1 fusion.57
  392.8 1.1 fusion.57
  394.0 1.1 fusion.57
  395.1 1.1 fusion.57
  396.3 1.1 fusion.57
  397.5 1.1 fusion.57
  398.7 1.1 fusion.57
  399.9 1.1 fusion.57
  401.1 1.1 fusion.57
  402.3 1.1 fusion.57
  403.5 1.1 fusion.57
  404.7 1.1 fusion.57
  405.9 1.1 fusion.57
  407.0 1.1 fusion.57
  408.2 0.0 copy-done.3
  408.2 1.0 fusion.10
  (24 shorter events, 0.2 us)
Async XLA Ops:
  6.5 1.6 copy-start
  6.5 326.1 %all-reduce.4.cloned.1.call-start = ((), (), s32[]{:S(2)}) async-start(), calls=%async_computation | async-start | bytes 524288 | tf_op jit(solution)/shard_map/psum | solution.py:77
  285.5 103.7 %all-gather.3.cloned.1.call-start = ((), (), s32[]{:S(2)}) async-start(), calls=%async_computation.1 | async-start | bytes 4456448 | tf_op jit(solution)/shard_map/all_gather | solution.py:102
  301.3 8.1 %copy-start.1 = (f32[1,128]{1,0:T(1,128)S(1)}, f32[1,128]{1,0:T(1,128)}, u32[]{:S(2)}) copy-start(f32[1,128]{1,0:T(1,128)} %param.14) | copy-start | bytes 1540
  301.3 15.7 %copy-start.2 = (f32[3,128]{1,0:T(4,128)S(1)}, f32[3,128]{1,0:T(4,128)}, u32[]{:S(2)}) copy-start(f32[3,128]{1,0:T(4,128)} %param.15) | copy-start | bytes 4612
  301.3 42.2 %copy-start.4 = (bf16[128,128]{1,0:T(8,128)(2,1)S(1)}, bf16[128,128]{1,0:T(8,128)(2,1)}, u32[]{:S(2)}) copy-start(bf16[128,128]{1,0:T(8,128)(2,1)} %param.16) | copy-start | bytes 98308
  301.3 106.9 %copy-start.3 = (f32[2,128]{1,0:T(2,128)S(1)}, f32[2,128]{1,0:T(2,128)}, u32[]{:S(2)}) copy-start(f32[2,128]{1,0:T(2,128)} %param.17) | copy-start | bytes 3076
  333.7 8.5 %collective-permute-start.1 = (bf16[1,512,128]{2,1,0:T(8,128)(2,1)S(1)}, bf16[1,512,128]{2,1,0:T(8,128)(2,1)S(1)}, u32[]{:S(2)}, u32[]{:S(2)}) collective-permute-start(bf16[1,512,128]{2,1,0:T(8,128)(2,1)S(1)} %divide_convert_fusion), channel_id=1, source_target_pairs={{4,0},{8,4},{12,8},{16,12},{20,16},{24,20},{28,24},{32,28},{36,32}... | collective-permute-start | bytes 393224 | tf_op jit(solution)/shard_map/ppermute | solution.py:18
  338.4 5.0 %collective-permute-start = (bf16[1,512,128]{2,1,0:T(8,128)(2,1)S(1)}, bf16[1,512,128]{2,1,0:T(8,128)(2,1)S(1)}, u32[]{:S(2)}, u32[]{:S(2)}) collective-permute-start(bf16[1,512,128]{2,1,0:T(8,128)(2,1)S(1)} %divide_convert_fusion), channel_id=1, source_target_pairs={{0,4},{4,8},{8,12},{12,16},{16,20},{20,24},{24,28},{28,32},{32,36}... | collective-permute-start | bytes 393224 | tf_op jit(solution)/shard_map/ppermute | solution.py:16
Sparse Core Ops, SparseCore 0:
  285.6 46.9 all-reduce.3
  344.6 44.5 all-gather.2
where the time goes:
time: 417 us; the launch traced here: 416 us
  blocking collectives  282 us (68%)
  waiting for transfers between devices  43.7 us (10%)
  other arithmetic  36.3 us (9%)
  local copies, waits for them, and re-layouts  19 us (5%)
  between operations  13.6 us (3%)
  matrix products  12.6 us (3%)
  starting transfers between devices  7.84 us (2%)
    psum x1, blocking collectives, local(): query_feats = lax.psum(contrib, ('tm', 'space')).astype(jnp.bfloat16)  250 us
    all_gather x1, waiting for transfers between devices, local(): lax.all_gather(carried[None], 'tm', axis=0, tiled=True)  26.2 us
    all_gather x1, blocking collectives, local(): lax.all_gather(retain_prod[None], 'tm', axis=0, tiled=True)  18.6 us
    select_n x16, other arithmetic, fold_step(): return jnp.where(source < position_tm, advanced, running)  18.4 us
    exp x1, local copies, waits for them, and re-layouts, local(): weights_exp = jnp.exp(scores - highest[:, None])  15.7 us
    psum x1, waiting for transfers between devices, local(): lax.psum((factor * totals, factor[..., None] * pos_sum, factor[..., None]...  15.6 us
    dot_general x1, matrix products, local(): jnp.dot(weights_exp.astype(jnp.bfloat16), frame_map, preferred_element_ty...  8.38 us
  transfers between devices with their start and end apart: 4, of which 4 were waited for; matrix products, arithmetic and copies ran while one was open for 6% of the time, Pallas kernels for 0%

commit v1 on v0

--- a/solution.py
+++ b/solution.py
@@ -42,7 +42,7 @@
         jnp.clip(local_frame, 0, frames_here - 1), jnp.clip(local_row, 0, rows_here - 1), query_col
     ]
     contrib = jnp.where(owned[:, None], picked.astype(jnp.float32), 0.0)
-    query_feats = lax.psum(contrib, ("tm", "space")).astype(jnp.bfloat16)
+    query_feats = lax.psum(lax.psum(contrib, "tm"), "space").astype(jnp.bfloat16)
     scale = 1.0 / math.sqrt(channels)
     col_coord = jnp.arange(map_width, dtype=jnp.int32).astype(jnp.float32) / map_width
     row_coord = (first_row + jnp.arange(rows_here, dtype=jnp.int32)).astype(

time: 417 us -> 316 us (0.76)
  blocking collectives: 282 us -> 48.7 us
  waiting for transfers between devices: 43.7 us -> 175 us
    psum x1, blocking collectives: 250 us -> 16.6 us  [local(): lax.psum(lax.psum(contrib, 'tm'), 'space').astype(jnp.bfloat16)]
    psum x0 -> x1, waiting for transfers between devices: none -> 112 us  [local(): lax.psum(contrib, 'tm')]
    psum x1, waiting for transfers between devices: 15.6 us -> 34.4 us  [local(): lax.psum((factor * totals, factor[..., None] * pos_sum, factor[..., None]...]
  transfers between devices with their start and end apart: 4 -> 5, of which waited for: 4 -> 5; matrix products, arithmetic and copies ran while one was open for 6% -> 3% of each run, Pallas kernels for 0% -> 0%
where the time goes in v1:
time: 316 us; the launch traced here: 315 us
  waiting for transfers between devices  175 us (55%)
  blocking collectives  48.7 us (15%)
  other arithmetic  37.7 us (12%)
  local copies, waits for them, and re-layouts  19.7 us (6%)
  between operations  13.2 us (4%)
  matrix products  12.6 us (4%)
  starting transfers between devices  7.88 us (2%)
    psum x1, waiting for transfers between devices, local(): lax.psum(contrib, 'tm')  112 us
    psum x1, waiting for transfers between devices, local(): lax.psum((factor * totals, factor[..., None] * pos_sum, factor[..., None]...  34.4 us
    all_gather x1, waiting for transfers between devices, local(): lax.all_gather(carried[None], 'tm', axis=0, tiled=True)  26.2 us
    all_gather x1, blocking collectives, local(): lax.all_gather(retain_prod[None], 'tm', axis=0, tiled=True)  18.6 us
    select_n x16, other arithmetic, fold_step(): return jnp.where(source < position_tm, advanced, running)  18.4 us
    psum x1, blocking collectives, local(): lax.psum(lax.psum(contrib, 'tm'), 'space').astype(jnp.bfloat16)  16.6 us
    exp x1, local copies, waits for them, and re-layouts, local(): weights_exp = jnp.exp(scores - highest[:, None])  15.6 us
    dot_general x1, matrix products, local(): jnp.dot(weights_exp.astype(jnp.bfloat16), frame_map, preferred_element_ty...  8.38 us
  transfers between devices with their start and end apart: 5, of which 5 were waited for; matrix products, arithmetic and copies ran while one was open for 3% of the time, Pallas kernels for 0%

profile of v1, /device:TPU:1, one launch (start us, length us, event | category | flops | bytes accessed | tf_op | source)
XLA Modules:
  0.0 315.0 jit_solution(7605456850292346576)
XLA Ops:
  6.5 0.0 copy-start
  6.5 0.0 all-reduce.5.cloned.1.call-start
  6.5 0.8 compare_and_fusion
  7.4 0.7 fusion.41
  8.1 0.0 copy-done
  8.1 3.1 gather_fusion
  11.3 0.8 convert_select_fusion
  12.1 0.0 all-reduce.5.cloned.1.call-update
  12.1 0.0 all-reduce.7.cloned.1.call-start
  12.2 0.7 subtract_bitcast_fusion
  12.8 0.8 slice_bitcast_fusion.2
  13.6 112.2 %all-reduce.5.cloned.1.call-done = f32[512,128]{1,0:T(8,128)} async-done(((f32[512,128]{1,0:T(8,128)}), f32[512,128]{1,0:T(8,128)}) %all-reduce.5.cloned.1.call-update) | async-done | bytes 262160 | tf_op jit(solution)/shard_map/psum | solution.py:45
  125.9 16.6 %all-reduce.8 = bf16[512,128]{1,0:T(8,128)(2,1)S(1)} all-reduce(f32[512,128]{1,0:T(8,128)} %all-reduce.5.cloned.1.call-done), channel_id=1, replica_groups=mesh['video'=4,'tm'=16,'space'=4] {'space'}, use_global_device_ids=true, to_apply=%region_1.2 | all-reduce | flops 65536 | bytes 393216 | tf_op jit(solution)/shard_map/psum | solution.py:45
  142.5 2.3 multiply_reduce_fusion
  144.8 7.0 %fusion.50 = (f32[512]{0:T(512)S(1)}, f32[512,7680]{1,0:T(8,128)}) fusion(f32[512]{0:T(512)S(1)} %get-tuple-element.139, f32[512,7680]{1,0:T(8,128)S(1)} %get-tuple-element.140), kind=kLoop, calls=%fused_computation.74 | loop fusion | flops 11795968 | bytes 31461376 | tf_op jit(solution)/shard_map/reduce_sum | solution.py:63
  151.8 6.1 %pmax.7 = f32[1,512]{1,0:T(1,128)S(1)} all-reduce(f32[1,512]{1,0:T(1,128)S(1)} %bitcast.66), channel_id=1, replica_groups=mesh['video'=4,'tm'=16,'space'=4] {'space'}, use_global_device_ids=true, to_apply=%region_3.4 | all-reduce | flops 512 | bytes 4096 | tf_op jit(solution)/shard_map/pmax | solution.py:75
  157.9 15.6 %copy.10 = f32[512,7680]{0,1:T(8,128)} copy(f32[512,7680]{1,0:T(8,128)} %get-tuple-element.135) | data formatting | bytes 31457280 | tf_op jit(solution)/shard_map/exp | solution.py:61
  173.5 0.0 copy-start.1
  173.5 0.0 copy-start.3
  173.5 8.4 %fusion.7 = f32[1,512,128]{2,1,0:T(8,128)} fusion(bf16[7680,128]{1,0:T(8,128)(2,1)S(1)} %bitcast.62, f32[512,7680]{1,0:T(8,128)} %get-tuple-element.135, f32[512]{0:T(512)S(1)} %bitcast.64), kind=kOutput, calls=%fused_computation.11 | convolution fusion | flops 1010630656 | bytes 17958912 | tf_op jit(solution)/shard_map/dot_general | solution.py:69
  181.9 0.0 copy-start.2
  181.9 0.0 all-reduce.7.cloned.1.call-update
  181.9 0.0 all-gather.3.cloned.1.call-start
  182.0 7.8 %fusion.48 = (f32[512,240]{0,1:T(8,128)S(1)}, f32[512,32]{0,1:T(8,128)S(1)}) fusion(f32[512,32,240]{0,2,1:T(8,128)} %bitcast.63), kind=kLoop, calls=%fused_computation.72 | loop fusion | flops 7725056 | bytes 16285696 | tf_op jit(solution)/shard_map/reduce_sum | solution.py:65
  189.8 0.1 multiply_reduce_fusion.1
  189.9 0.1 multiply_reduce_fusion.2
  190.0 7.5 %all-reduce = (f32[512]{0:T(512)S(1)}, f32[1,512,2]{1,2,0:T(2,128)S(1)}) all-reduce(f32[512]{0:T(512)S(1)} %bitcast.70, f32[1,512,2]{1,2,0:T(2,128)S(1)} %maximum_multiply_fusion), channel_id=1, replica_groups=mesh['video'=4,'tm'=16,'space'=4] {'space'}, use_global_device_ids=true, to_apply=%region_10.11 | all-reduce | flops 1536 | bytes 12288 | tf_op jit(solution)/shard_map/psum | solution.py:77
  197.5 34.4 %all-reduce.7.cloned.1.call-done = f32[1,512,128]{2,1,0:T(8,128)} async-done(((f32[1,512,128]{2,1,0:T(8,128)}), f32[1,512,128]{2,1,0:T(8,128)}) %all-reduce.7.cloned.1.call-update) | async-done | bytes 262160 | tf_op jit(solution)/shard_map/psum | solution.py:77
  231.9 1.1 divide_convert_fusion
  233.0 4.7 %collective-permute-start.1 = (bf16[1,512,128]{2,1,0:T(8,128)(2,1)S(1)}, bf16[1,512,128]{2,1,0:T(8,128)(2,1)S(1)}, u32[]{:S(2)}, u32[]{:S(2)}) collective-permute-start(bf16[1,512,128]{2,1,0:T(8,128)(2,1)S(1)} %divide_convert_fusion), channel_id=1, source_target_pairs={{4,0},{8,4},{12,8},{16,12},{20,16},{24,20},{28,24},{32,28},{36,32}... | collective-permute-start | bytes 393224 | tf_op jit(solution)/shard_map/ppermute | solution.py:18
  237.7 3.1 collective-permute-start
  240.8 0.0 copy-done.1
  240.8 0.7 collective-permute-done.1
  241.5 1.2 collective-permute-done
  242.7 0.1 maximum_convert_fusion
  242.8 0.0 copy-done.3
  242.8 0.9 multiply_add_fusion
  243.7 0.0 all-gather.3.cloned.1.call-update
  243.8 18.6 %all-gather = f32[16,1,128]{2,1,0:T(1,128)S(1)} all-gather(f32[1,1,128]{2,1,0:T(1,128)S(1)} %bitcast.73), channel_id=1, replica_groups=mesh['video'=4,'tm'=16,'space'=4] {'tm'}, dimensions={0}, use_global_device_ids=true | all-gather | bytes 8704 | tf_op jit(solution)/shard_map/all_gather | solution.py:101
  262.3 26.2 %all-gather.3.cloned.1.call-done = f32[16,512,128]{2,1,0:T(8,128)} async-done(((f32[1,512,128]{2,1,0:T(8,128)}), f32[16,512,128]{2,1,0:T(8,128)}) %all-gather.3.cloned.1.call-update) | async-done | bytes 4194320 | tf_op jit(solution)/shard_map/all_gather | solution.py:102
  288.5 19.0 %while.14 = (s32[]{:T(128)}, f32[512,128]{1,0:T(8,128)S(1)}, s32[]{:T(128)}, f32[16,128]{1,0:T(8,128)S(1)}, f32[16,512,128]{2,1,0:T(8,128)}, /*index=5*/s32[]{:T(128)}, s32[]{:T(128)}) while((s32[]{:T(128)}, f32[512,128]{1,0:T(8,128)S(1)}, s32[]{:T(128)}, f32[16,128]{1,0:T(8,128)S(1)}, f32[16,512,128]{2,1,0:T(8,128)}, ...), condition=%wide.region_13.14_spmd.clone, body=%wide.region_12.13_spmd.clone.sunk | while | flops 262148 | bytes 788081 | solution.py:110
  288.5 1.1 fusion.57
  289.7 1.1 fusion.57
  290.9 1.1 fusion.57
  292.1 1.1 fusion.57
  293.3 1.1 fusion.57
  294.4 1.1 fusion.57
  295.6 1.1 fusion.57
  296.8 1.1 fusion.57
  298.0 1.1 fusion.57
  299.2 1.1 fusion.57
  300.4 1.1 fusion.57
  301.6 1.1 fusion.57
  302.8 1.1 fusion.57
  304.0 1.1 fusion.57
  305.1 1.1 fusion.57
  306.3 1.1 fusion.57
  307.5 0.0 copy-done.2
  307.5 1.0 fusion.10
  (22 shorter events, 0.2 us)
Async XLA Ops:
  6.5 1.6 copy-start
  6.5 119.3 %all-reduce.5.cloned.1.call-start = ((), (), s32[]{:S(2)}) async-start(), calls=%async_computation | async-start | bytes 524288 | tf_op jit(solution)/shard_map/psum | solution.py:45
  12.1 219.8 %all-reduce.7.cloned.1.call-start = ((), (), s32[]{:S(2)}) async-start(), calls=%async_computation.1 | async-start | bytes 524288 | tf_op jit(solution)/shard_map/psum | solution.py:77
  173.5 67.3 %copy-start.1 = (f32[1,128]{1,0:T(1,128)S(1)}, f32[1,128]{1,0:T(1,128)}, u32[]{:S(2)}) copy-start(f32[1,128]{1,0:T(1,128)} %param.14) | copy-start | bytes 1540
  173.5 69.3 %copy-start.3 = (bf16[128,128]{1,0:T(8,128)(2,1)S(1)}, bf16[128,128]{1,0:T(8,128)(2,1)}, u32[]{:S(2)}) copy-start(bf16[128,128]{1,0:T(8,128)(2,1)} %param.16) | copy-start | bytes 98308
  181.9 125.6 %copy-start.2 = (f32[2,128]{1,0:T(2,128)S(1)}, f32[2,128]{1,0:T(2,128)}, u32[]{:S(2)}) copy-start(f32[2,128]{1,0:T(2,128)} %param.17) | copy-start | bytes 3076
  181.9 106.6 %all-gather.3.cloned.1.call-start = ((), (), s32[]{:S(2)}) async-start(), calls=%async_computation.2 | async-start | bytes 4456448 | tf_op jit(solution)/shard_map/all_gather | solution.py:102
  233.0 8.5 %collective-permute-start.1 = (bf16[1,512,128]{2,1,0:T(8,128)(2,1)S(1)}, bf16[1,512,128]{2,1,0:T(8,128)(2,1)S(1)}, u32[]{:S(2)}, u32[]{:S(2)}) collective-permute-start(bf16[1,512,128]{2,1,0:T(8,128)(2,1)S(1)} %divide_convert_fusion), channel_id=1, source_target_pairs={{4,0},{8,4},{12,8},{16,12},{20,16},{24,20},{28,24},{32,28},{36,32}... | collective-permute-start | bytes 393224 | tf_op jit(solution)/shard_map/ppermute | solution.py:18
  237.7 5.0 %collective-permute-start = (bf16[1,512,128]{2,1,0:T(8,128)(2,1)S(1)}, bf16[1,512,128]{2,1,0:T(8,128)(2,1)S(1)}, u32[]{:S(2)}, u32[]{:S(2)}) collective-permute-start(bf16[1,512,128]{2,1,0:T(8,128)(2,1)S(1)} %divide_convert_fusion), channel_id=1, source_target_pairs={{0,4},{4,8},{8,12},{12,16},{16,20},{20,24},{24,28},{28,32},{32,36}... | collective-permute-start | bytes 393224 | tf_op jit(solution)/shard_map/ppermute | solution.py:16
Sparse Core Ops, SparseCore 0:
  12.2 113.5 all-reduce.4
  182.0 49.7 all-reduce.6
  243.9 44.5 all-gather.2
